TPU v7x, 32 devices: a whole 2x2x4 slice. The times are simulated.
32 devices in a mesh: cuts: 2 (over y), idx: 8 (over z, x), half: 2 (over core).
Axes of the slice: x: 2, y: 2, z: 4, core: 2. Of those that a mesh axis runs over, the one named last changes fastest.
Arguments:
- left_factor: float32 [2, 4, 64, 1024, 256], P('half', 'cuts', 'idx'), parts along dimension 1, may hold values from -6 to 6
- right_factor: float32 [2, 4, 64, 256, 1024], P('half', 'cuts', None, 'idx'), parts along dimension 1, may hold values from -0.25 to 0.25
Outputs:
- amplitudes: float32 [1024, 4, 1024], P(('idx', 'half'), 'cuts'), parts along dimension 1
There are 2 independent parts, one for each index of `cuts`. A program takes and returns all parts, laid end to end along the dimension named above; each array names one. Nothing has to cross between parts.
All inputs are finite; a program needn't handle non-finite values.
Results may differ from a plain program's by a relative error of at most 0.0003.
Values sent between devices are 32-bit elements; how exact they have to be, the bound alone decides.
A program may use at most 256 MiB of HBM per device.

v0:
```python
import math
import jax
import jax.numpy as jnp
from jax import lax
from jax.sharding import PartitionSpec as P

BATCH = 64
N = 1024


def swapped(x, axis, bit):
    return lax.ppermute(x, axis, [(i, i ^ 1 << bit) for i in range(lax.axis_size(axis))])


def complex_product(left_real, left_imag, right_real, right_imag, pattern):
    highest = lax.Precision.HIGHEST
    first_term = jnp.einsum(pattern, left_real, right_real, precision=highest)
    second_term = jnp.einsum(pattern, left_imag, right_imag, precision=highest)
    mixed_term = jnp.einsum(
        pattern, left_real + left_imag, right_real + right_imag, precision=highest
    )
    return (first_term - second_term, mixed_term - first_term - second_term)


def on_device(left_factor, right_factor):
    left_local = left_factor[0]
    right_local = right_factor[0]
    columns = lax.all_to_all(right_local, "idx", split_axis=1, concat_axis=2, tiled=True)
    real_part, imag_part = complex_product(
        left_local[0], left_local[1], columns[0], columns[1], "bmk,bkn->bmn"
    )
    merged = jnp.stack([real_part, imag_part])
    half_cols = merged.shape[3] // 2
    half_index = lax.axis_index("half")
    outgoing = lax.dynamic_slice_in_dim(merged, (1 - half_index) * half_cols, half_cols, 3)
    own_slab = lax.dynamic_slice_in_dim(merged, half_index * half_cols, half_cols, 3)
    other_slab = swapped(outgoing, "half", 0)
    is_lower = half_index == 0
    first_pair = jnp.where(is_lower, own_slab, other_slab)
    second_pair = jnp.where(is_lower, other_slab, own_slab)
    norm_scale = 1.0 / math.sqrt(2.0 * BATCH * N)
    real_part, imag_part = complex_product(
        first_pair[0], first_pair[1], second_pair[0], second_pair[1], "bmn,bon->mo"
    )
    return lax.psum_scatter(
        jnp.stack([real_part, imag_part], axis=1) * norm_scale,
        ("idx", "half"),
        scatter_dimension=0,
        tiled=True,
    )


def solution(mesh):
    return jax.shard_map(
        on_device,
        mesh=mesh,
        in_specs=(P("half", "cuts", "idx", None, None), P("half", "cuts", None, "idx", None)),
        out_specs=P(("idx", "half"), "cuts", None),
        check_vma=False,
    )
```

profile of v0, /device:TPU:0, one launch (start us, length us, event | category | flops | bytes accessed | tf_op | source)
XLA Modules:
  0.0 989.9 jit_solution(9931853911004770356)
XLA Ops:
  6.5 11.8 %copy.11 = f32[1,2,64,32,1024]{4,3,1,2,0:T(8,128)} copy(f32[1,2,64,32,1024]{4,3,2,1,0:T(8,128)} %param.3) | data formatting | bytes 33554432 | tf_op args[1]
  18.3 7.3 all-to-all-start
  25.6 0.0 reduce-scatter.2.cloned.1.call-start
  25.7 363.0 %all-to-all-done = f32[2,64,32,1024]{3,2,0,1:T(8,128)} async-done(((f32[2,64,32,1024]{3,2,0,1:T(8,128)}), f32[2,64,32,1024]{3,2,0,1:T(8,128)}, u32[]{:S(2)}, u32[]{:S(2)}) %all-to-all-start) | async-done | bytes 16777248 | tf_op jit(solution)/shard_map/all_to_all | solution.py:28
  388.7 11.8 %copy.10 = f32[2,8,8,32,1024]{4,3,1,2,0:T(8,128)} copy(f32[2,8,8,32,1024]{4,3,0,2,1:T(8,128)} %bitcast.2) | data formatting | bytes 33554432 | tf_op jit(solution)/shard_map/all_to_all | solution.py:28
  400.5 6.7 fusion.38
  407.2 0.0 copy-start.1
  407.2 0.0 copy-start
  407.3 34.2 %fusion.24 = f32[8,1024,1024]{2,1,0:T(8,128)} fusion(f32[8,256,1024]{2,1,0:T(8,128)S(1)} %bitcast.103, f32[1,2,8,1024,256]{4,3,2,1,0:T(8,128)} %param.2), kind=kOutput, calls=%fused_computation.36 | convolution fusion | flops 25769803776 | bytes 50331648 | tf_op jit(solution)/shard_map/bmk,bkn->bmn/dot_general | solution.py:17
  441.5 0.0 copy-done.1
  441.5 0.0 copy-done
  441.5 32.8 %fusion.21 = f32[8,1024,1024]{2,1,0:T(8,128)} fusion(f32[8,256,1024]{2,1,0:T(8,128)S(1)} %bitcast.101, f32[1,2,8,1024,256]{4,3,2,1,0:T(8,128)} %param.2), kind=kOutput, calls=%fused_computation.33 | convolution fusion | flops 25769803776 | bytes 50331648 | tf_op jit(solution)/shard_map/bmk,bkn->bmn/dot_general | solution.py:18
  474.3 55.7 %subtract_bitcast_fusion = f32[1,8,1024,1024]{3,2,1,0:T(8,128)} fusion(f32[8,1024,1024]{2,1,0:T(8,128)} %fusion.21, f32[8,1024,1024]{2,1,0:T(8,128)} %fusion.24, f32[8,256,1024]{2,1,0:T(8,128)} %bitcast.104, f32[8,256,1024]{2,1,0:T(8,128)} %bitcast.102, f32[1,2,8,1024,256]{4,3,2,1,0:T(8,128)} %param.2), kind=kOutput, calls=%fused_computation.6 | convolution fusion | flops 25790775296 | bytes 134217728 | tf_op jit(solution)/shard_map/bmk,bkn->bmn/dot_general | solution.py:19
  530.0 33.0 %subtract_bitcast_fusion.1 = f32[1,8,1024,1024]{3,2,1,0:T(8,128)} fusion(f32[8,1024,1024]{2,1,0:T(8,128)} %fusion.24, f32[8,1024,1024]{2,1,0:T(8,128)} %fusion.21), kind=kLoop, calls=%fused_computation.7 | loop fusion | flops 8388608 | bytes 100663296 | tf_op jit(solution)/shard_map/stack | solution.py:32
  563.0 23.0 %fusion = f32[2,8,1024,512]{3,2,1,0:T(8,128)} fusion(s32[]{:T(128)S(6)} %select_n.20, f32[1,8,1024,1024]{3,2,1,0:T(8,128)} %subtract_bitcast_fusion.1, f32[1,8,1024,1024]{3,2,1,0:T(8,128)} %subtract_bitcast_fusion), kind=kLoop, calls=%fused_computation.4 | loop fusion | flops 8388608 | bytes 100663296 | tf_op jit(solution)/shard_map/stack | solution.py:32
  586.0 0.0 collective-permute-start
  586.0 49.5 %collective-permute-done = f32[2,8,1024,512]{3,2,1,0:T(8,128)} collective-permute-done((f32[2,8,1024,512]{3,2,1,0:T(8,128)}, f32[2,8,1024,512]{3,2,1,0:T(8,128)}, u32[]{:S(2)}, u32[]{:S(2)}) %collective-permute-start) | collective-permute-done | bytes 33554464 | tf_op jit(solution)/shard_map/ppermute | solution.py:12
  635.5 54.2 %broadcast_select_fusion.1 = (f32[2,8,1024,512]{3,2,1,0:T(8,128)}, f32[2,8,1024,512]{3,2,1,0:T(8,128)}) fusion(f32[2,8,1024,512]{3,2,1,0:T(8,128)} %collective-permute-done, pred[]{:T(512)S(6)} %eq.3, s32[]{:T(128)S(6)} %select_n.19, f32[1,8,1024,1024]{3,2,1,0:T(8,128)} %subtract_bitcast_fusion, f32[1,8,1024,1024]{3,2,1,0:T(8,128)} %subtract_bitcast_fusion.1), kind=kLoop, calls=%fused_computation.22 | loop fusion | flops 33554432 | bytes 167772160 | tf_op jit(solution)/shard_map/jit(_where)/select_n | solution.py:39
  689.7 59.4 %fusion.5 = f32[1024,1024,1]{1,0,2:T(8,128)S(1)} fusion(f32[2,8,1024,512]{3,2,1,0:T(8,128)} %get-tuple-element.6, f32[2,8,1024,512]{3,2,1,0:T(8,128)} %get-tuple-element.5), kind=kOutput, calls=%fused_computation.11 | convolution fusion | flops 51539607552 | bytes 37748736 | tf_op jit(solution)/shard_map/bmn,bon->mo/dot_general | solution.py:18
  749.1 59.3 %fusion.8 = f32[1024,1024,1]{1,0,2:T(8,128)S(1)} fusion(f32[2,8,1024,512]{3,2,1,0:T(8,128)} %get-tuple-element.6, f32[2,8,1024,512]{3,2,1,0:T(8,128)} %get-tuple-element.5), kind=kOutput, calls=%fused_computation.14 | convolution fusion | flops 51539607552 | bytes 37748736 | tf_op jit(solution)/shard_map/bmn,bon->mo/dot_general | solution.py:17
  808.4 63.7 %fusion.32 = f32[1024,1,1024]{2,0,1:T(8,128)S(1)} fusion(f32[1024,1024,1]{1,0,2:T(8,128)S(1)} %fusion.5, f32[1024,1024,1]{1,0,2:T(8,128)S(1)} %fusion.8, f32[2,8,1024,512]{3,2,1,0:T(8,128)} %get-tuple-element.6, f32[2,8,1024,512]{3,2,1,0:T(8,128)} %get-tuple-element.5), kind=kOutput, calls=%fused_computation.45 | convolution fusion | flops 51550093312 | bytes 79691776 | tf_op jit(solution)/shard_map/bmn,bon->mo/dot_general | solution.py:19
  872.1 1.4 fusion.33
  873.5 4.3 maximum_multiply_fusion
  877.7 0.0 reduce-scatter.2.cloned.1.call-update
  877.8 102.6 %reduce-scatter.2.cloned.1.call-done = f32[64,2,1024]{2,0,1:T(8,128)} async-done(((f32[1024,2,1024]{2,0,1:T(8,128)}), f32[64,2,1024]{2,0,1:T(8,128)}) %reduce-scatter.2.cloned.1.call-update) | async-done | bytes 524304 | tf_op jit(solution)/shard_map/reduce_scatter | solution.py:45
  980.4 2.2 copy.7
Async XLA Ops:
  18.3 370.3 %all-to-all-start = ((f32[2,64,32,1024]{3,2,0,1:T(8,128)}), f32[2,64,32,1024]{3,2,0,1:T(8,128)}, u32[]{:S(2)}, u32[]{:S(2)}) async-start(f32[2,64,32,1024]{3,2,0,1:T(8,128)} %bitcast.105), calls=%async_computation | async-start | bytes 33554432 | tf_op jit(solution)/shard_map/all_to_all | solution.py:28
  25.6 954.7 %reduce-scatter.2.cloned.1.call-start = ((), (), s32[]{:S(2)}) async-start(), calls=%async_computation.2 | async-start | bytes 8912896 | tf_op jit(solution)/shard_map/reduce_scatter | solution.py:45
  407.2 34.3 %copy-start.1 = (f32[1,8,8,32,1024]{4,3,2,1,0:T(8,128)}, f32[1,8,8,32,1024]{4,3,2,1,0:T(8,128)S(1)}, u32[]{:S(2)}) copy-start(f32[1,8,8,32,1024]{4,3,2,1,0:T(8,128)S(1)} %get-tuple-element.8) | copy-start | bytes 25165828
  407.2 34.3 %copy-start = (f32[1,8,8,32,1024]{4,3,2,1,0:T(8,128)}, f32[1,8,8,32,1024]{4,3,2,1,0:T(8,128)S(1)}, u32[]{:S(2)}) copy-start(f32[1,8,8,32,1024]{4,3,2,1,0:T(8,128)S(1)} %get-tuple-element.7) | copy-start | bytes 25165828
  586.0 49.5 %collective-permute-start = (f32[2,8,1024,512]{3,2,1,0:T(8,128)}, f32[2,8,1024,512]{3,2,1,0:T(8,128)}, u32[]{:S(2)}, u32[]{:S(2)}) collective-permute-start(f32[2,8,1024,512]{3,2,1,0:T(8,128)} %fusion), channel_id=1, source_target_pairs={{0,1},{1,0},{2,3},{3,2},{4,5},{5,4},{6,7},{7,6},{8,9},{9,8},{10,11... | collective-permute-start | bytes 100663304 | tf_op jit(solution)/shard_map/ppermute | solution.py:12
Sparse Core Ops, SparseCore 0:
  877.9 102.4 reduce-scatter.1
where the time goes:
time: 997 us; the launch traced here: 990 us
  waiting for transfers between devices  515 us (52%)
  matrix products  305 us (31%)
  other arithmetic  116 us (12%)
  local copies, waits for them, and re-layouts  32.6 us (3%)
  between operations  13.9 us (1%)
    all_to_all x1, waiting for transfers between devices, on_device(): lax.all_to_all(right_local, 'idx', split_axis=1, concat_axis=2, tiled=True)  363 us
    dot_general x2, matrix products, complex_product(): jnp.einsum(pattern, left_real + left_imag, right_real + right_imag, preci...  119 us
    reduce_scatter x1, waiting for transfers between devices, on_device(): lax.psum_scatter(jnp.stack([real_part, imag_part], axis=1) * norm_scale,...  103 us
    dot_general x2, matrix products, complex_product(): first_term = jnp.einsum(pattern, left_real, right_real, precision=highest)  93.6 us
    dot_general x2, matrix products, complex_product(): second_term = jnp.einsum(pattern, left_imag, right_imag, precision=highest)  92.2 us
    another operation x2, other arithmetic, on_device(): merged = jnp.stack([real_part, imag_part])  56 us
    select_n x1, other arithmetic, on_device(): first_pair = jnp.where(is_lower, own_slab, other_slab)  54.2 us
    ppermute x1, waiting for transfers between devices, swapped(): lax.ppermute(x, axis, [(i, i ^ 1 << bit) for i in range(lax.axis_size(axi...  49.5 us
  transfers between devices with their start and end apart: 3, of which 3 were waited for; matrix products, arithmetic and copies ran while one was open for 0% of the time, Pallas kernels for 0%

commit v1 on v0

--- a/solution.py
+++ b/solution.py
@@ -25,7 +25,12 @@
 def on_device(left_factor, right_factor):
     left_local = left_factor[0]
     right_local = right_factor[0]
-    columns = lax.all_to_all(right_local, "idx", split_axis=1, concat_axis=2, tiled=True)
+    columns = jnp.concatenate(
+        lax.all_to_all(
+            jnp.stack(jnp.split(right_local, lax.axis_size("idx"), axis=1)), "idx", 0, 0
+        ),
+        axis=2,
+    )
     real_part, imag_part = complex_product(
         left_local[0], left_local[1], columns[0], columns[1], "bmk,bkn->bmn"
     )

time: 997 us -> 1070 us (1.073)
  matrix products: 305 us -> 367 us
    dot_general x2, matrix products: 92.2 us -> 126 us  [complex_product(): second_term = jnp.einsum(pattern, left_imag, right_imag, precision=highest)]
    dot_general x2, matrix products: 93.6 us -> 124 us  [complex_product(): first_term = jnp.einsum(pattern, left_real, right_real, precision=highest)]
where the time goes in v1:
time: 1070 us; the launch traced here: 1060 us
  waiting for transfers between devices  515 us (48%)
  matrix products  367 us (34%)
  other arithmetic  118 us (11%)
  local copies, waits for them, and re-layouts  40.5 us (4%)
  between operations  13.7 us (1%)
    all_to_all x1, waiting for transfers between devices, on_device(): lax.all_to_all(jnp.stack(jnp.split(right_local, lax.axis_size('idx'), axi...  363 us
    dot_general x2, matrix products, complex_product(): second_term = jnp.einsum(pattern, left_imag, right_imag, precision=highest)  126 us
    dot_general x2, matrix products, complex_product(): first_term = jnp.einsum(pattern, left_real, right_real, precision=highest)  124 us
    dot_general x2, matrix products, complex_product(): jnp.einsum(pattern, left_real + left_imag, right_real + right_imag, preci...  117 us
    reduce_scatter x1, waiting for transfers between devices, on_device(): lax.psum_scatter(jnp.stack([real_part, imag_part], axis=1) * norm_scale,...  103 us
    another operation x2, other arithmetic, on_device(): merged = jnp.stack([real_part, imag_part])  56.5 us
    select_n x1, other arithmetic, on_device(): first_pair = jnp.where(is_lower, own_slab, other_slab)  56.2 us
    ppermute x1, waiting for transfers between devices, swapped(): lax.ppermute(x, axis, [(i, i ^ 1 << bit) for i in range(lax.axis_size(axi...  49.5 us
  transfers between devices with their start and end apart: 3, of which 3 were waited for; matrix products, arithmetic and copies ran while one was open for 0% of the time, Pallas kernels for 0%

profile of v1, /device:TPU:0, one launch (start us, length us, event | category | flops | bytes accessed | tf_op | source)
XLA Modules:
  0.0 1062.0 jit_solution(4471487021576950861)
XLA Ops:
  6.5 0.0 copy-start.2
  6.5 3.3 fusion.47
  9.9 3.9 fusion.46
  13.8 3.5 fusion.45
  17.2 3.2 fusion.44
  20.4 0.0 copy-done.2
  20.4 1.5 fusion.43
  21.9 1.5 fusion.42
  23.4 1.5 fusion.41
  24.9 1.4 fusion.40
  26.3 7.3 all-to-all-start
  33.6 0.0 reduce-scatter.2.cloned.1.call-start
  33.6 363.0 %all-to-all-done = f32[8,2,8,32,1024]{4,3,2,1,0:T(8,128)} async-done(((f32[8,2,8,32,1024]{4,3,2,1,0:T(8,128)}), f32[8,2,8,32,1024]{4,3,2,1,0:T(8,128)}, u32[]{:S(2)}, u32[]{:S(2)}) %all-to-all-start) | async-done | bytes 16777248 | tf_op jit(solution)/shard_map/all_to_all | solution.py:29
  396.6 11.8 %copy.52 = f32[8,2,8,32,1024]{4,3,0,2,1:T(8,128)} copy(f32[8,2,8,32,1024]{4,3,2,1,0:T(8,128)} %all-to-all-done) | data formatting | bytes 33554432 | tf_op jit(solution)/shard_map/all_to_all | solution.py:29
  408.5 6.7 fusion.48
  415.2 0.0 copy-start.1
  415.2 0.0 copy-start
  415.2 63.1 %fusion.23 = f32[8,1024,1024]{2,1,0:T(8,128)} fusion(f32[8,256,1024]{2,1,0:T(8,128)S(1)} %bitcast.148, f32[1,2,8,1024,256]{4,3,2,1,0:T(8,128)} %param.2), kind=kOutput, calls=%fused_computation.35 | convolution fusion | flops 25769803776 | bytes 50331648 | tf_op jit(solution)/shard_map/bmk,bkn->bmn/dot_general | solution.py:18
  478.3 0.0 copy-done.1
  478.3 0.0 copy-done
  478.3 61.5 %fusion.26 = f32[8,1024,1024]{2,1,0:T(8,128)} fusion(f32[8,256,1024]{2,1,0:T(8,128)S(1)} %bitcast.146, f32[1,2,8,1024,256]{4,3,2,1,0:T(8,128)} %param.2), kind=kOutput, calls=%fused_computation.38 | convolution fusion | flops 25769803776 | bytes 50331648 | tf_op jit(solution)/shard_map/bmk,bkn->bmn/dot_general | solution.py:17
  539.9 51.7 %fusion.3 = f32[1,8,1024,1024]{2,3,1,0:T(8,128)} fusion(f32[8,1024,1024]{2,1,0:T(8,128)} %fusion.23, f32[8,1024,1024]{2,1,0:T(8,128)} %fusion.26, f32[8,256,1024]{2,1,0:T(8,128)} %bitcast.147, f32[8,256,1024]{2,1,0:T(8,128)} %bitcast.149, f32[1,2,8,1024,256]{4,3,2,1,0:T(8,128)} %param.2), kind=kOutput, calls=%fused_computation.9 | convolution fusion | flops 25790775296 | bytes 134217728 | tf_op jit(solution)/shard_map/bmk,bkn->bmn/dot_general | solution.py:19
  591.6 33.0 %fusion.2 = f32[1,8,1024,1024]{2,3,1,0:T(8,128)} fusion(f32[8,1024,1024]{2,1,0:T(8,128)} %fusion.23, f32[8,1024,1024]{2,1,0:T(8,128)} %fusion.26), kind=kLoop, calls=%fused_computation.8 | loop fusion | flops 8388608 | bytes 100663296 | tf_op jit(solution)/shard_map/stack | solution.py:37
  624.6 23.5 %fusion = f32[2,8,1024,512]{2,3,1,0:T(8,128)} fusion(s32[]{:T(128)S(6)} %select_n.20, f32[1,8,1024,1024]{2,3,1,0:T(8,128)} %fusion.2, f32[1,8,1024,1024]{2,3,1,0:T(8,128)} %fusion.3), kind=kLoop, calls=%fused_computation.4 | loop fusion | flops 8388608 | bytes 100663296 | tf_op jit(solution)/shard_map/stack | solution.py:37
  648.1 0.0 collective-permute-start
  648.1 49.5 %collective-permute-done = f32[2,8,1024,512]{2,3,1,0:T(8,128)} collective-permute-done((f32[2,8,1024,512]{2,3,1,0:T(8,128)}, f32[2,8,1024,512]{2,3,1,0:T(8,128)}, u32[]{:S(2)}, u32[]{:S(2)}) %collective-permute-start) | collective-permute-done | bytes 33554464 | tf_op jit(solution)/shard_map/ppermute | solution.py:12
  697.6 56.2 %broadcast_select_fusion.1 = (f32[2,8,1024,512]{2,3,1,0:T(8,128)}, f32[2,8,1024,512]{2,3,1,0:T(8,128)}) fusion(f32[2,8,1024,512]{2,3,1,0:T(8,128)} %collective-permute-done, pred[]{:T(512)S(6)} %eq.3, s32[]{:T(128)S(6)} %select_n.19, f32[1,8,1024,1024]{2,3,1,0:T(8,128)} %fusion.3, f32[1,8,1024,1024]{2,3,1,0:T(8,128)} %fusion.2), kind=kLoop, calls=%fused_computation.24 | loop fusion | flops 33554432 | bytes 167772160 | tf_op jit(solution)/shard_map/jit(_where)/select_n | solution.py:44
  753.8 62.5 %fusion.7 = f32[1024,1024,1]{1,0,2:T(8,128)S(1)} fusion(f32[2,8,1024,512]{2,3,1,0:T(8,128)} %get-tuple-element.6, f32[2,8,1024,512]{2,3,1,0:T(8,128)} %get-tuple-element.5), kind=kOutput, calls=%fused_computation.14 | convolution fusion | flops 51539607552 | bytes 37748736 | tf_op jit(solution)/shard_map/bmn,bon->mo/dot_general | solution.py:18
  816.3 62.5 %fusion.10 = f32[1024,1024,1]{1,0,2:T(8,128)S(1)} fusion(f32[2,8,1024,512]{2,3,1,0:T(8,128)} %get-tuple-element.6, f32[2,8,1024,512]{2,3,1,0:T(8,128)} %get-tuple-element.5), kind=kOutput, calls=%fused_computation.17 | convolution fusion | flops 51539607552 | bytes 37748736 | tf_op jit(solution)/shard_map/bmn,bon->mo/dot_general | solution.py:17
  878.8 65.6 %fusion.34 = f32[1024,1,1024]{2,0,1:T(8,128)S(1)} fusion(f32[1024,1024,1]{1,0,2:T(8,128)S(1)} %fusion.7, f32[1024,1024,1]{1,0,2:T(8,128)S(1)} %fusion.10, f32[2,8,1024,512]{2,3,1,0:T(8,128)} %get-tuple-element.6, f32[2,8,1024,512]{2,3,1,0:T(8,128)} %get-tuple-element.5), kind=kOutput, calls=%fused_computation.47 | convolution fusion | flops 51550093312 | bytes 79691776 | tf_op jit(solution)/shard_map/bmn,bon->mo/dot_general | solution.py:19
  944.4 1.4 fusion.35
  945.8 4.3 maximum_multiply_fusion
  950.0 0.0 reduce-scatter.2.cloned.1.call-update
  950.0 102.6 %reduce-scatter.2.cloned.1.call-done = f32[64,2,1024]{2,0,1:T(8,128)} async-done(((f32[1024,2,1024]{2,0,1:T(8,128)}), f32[64,2,1024]{2,0,1:T(8,128)}) %reduce-scatter.2.cloned.1.call-update) | async-done | bytes 524304 | tf_op jit(solution)/shard_map/reduce_scatter | solution.py:50
  1052.6 2.2 copy.41
Async XLA Ops:
  6.5 13.9 %copy-start.2 = (f32[1,2,64,32,1024]{4,3,2,1,0:T(8,128)S(1)}, f32[1,2,64,32,1024]{4,3,2,1,0:T(8,128)}, u32[]{:S(2)}) copy-start(f32[1,2,64,32,1024]{4,3,2,1,0:T(8,128)} %param.3) | copy-start | bytes 50331652
  26.3 370.4 %all-to-all-start = ((f32[8,2,8,32,1024]{4,3,2,1,0:T(8,128)}), f32[8,2,8,32,1024]{4,3,2,1,0:T(8,128)}, u32[]{:S(2)}, u32[]{:S(2)}) async-start(f32[8,2,8,32,1024]{4,3,2,1,0:T(8,128)} %fusion.40), calls=%async_computation | async-start | bytes 33554432 | tf_op jit(solution)/shard_map/all_to_all | solution.py:29
  33.6 1019.1 %reduce-scatter.2.cloned.1.call-start = ((), (), s32[]{:S(2)}) async-start(), calls=%async_computation.2 | async-start | bytes 8912896 | tf_op jit(solution)/shard_map/reduce_scatter | solution.py:50
  415.2 63.1 %copy-start.1 = (f32[1,8,8,32,1024]{4,3,2,1,0:T(8,128)}, f32[1,8,8,32,1024]{4,3,2,1,0:T(8,128)S(1)}, u32[]{:S(2)}) copy-start(f32[1,8,8,32,1024]{4,3,2,1,0:T(8,128)S(1)} %get-tuple-element.8) | copy-start | bytes 25165828
  415.2 63.1 %copy-start = (f32[1,8,8,32,1024]{4,3,2,1,0:T(8,128)}, f32[1,8,8,32,1024]{4,3,2,1,0:T(8,128)S(1)}, u32[]{:S(2)}) copy-start(f32[1,8,8,32,1024]{4,3,2,1,0:T(8,128)S(1)} %get-tuple-element.7) | copy-start | bytes 25165828
  648.1 49.5 %collective-permute-start = (f32[2,8,1024,512]{2,3,1,0:T(8,128)}, f32[2,8,1024,512]{2,3,1,0:T(8,128)}, u32[]{:S(2)}, u32[]{:S(2)}) collective-permute-start(f32[2,8,1024,512]{2,3,1,0:T(8,128)} %fusion), channel_id=1, source_target_pairs={{0,1},{1,0},{2,3},{3,2},{4,5},{5,4},{6,7},{7,6},{8,9},{9,8},{10,11... | collective-permute-start | bytes 100663304 | tf_op jit(solution)/shard_map/ppermute | solution.py:12
Sparse Core Ops, SparseCore 0:
  950.2 102.4 reduce-scatter.1
